TPU v7x, 128 devices: a whole 4x4x4 slice. The times are simulated.
128 devices in a mesh: wide: 16 (over z_hi, x, core), narrow: 8 (over z_lo, y).
Axes of the slice: x: 4, y: 4, z: 4 (z_hi: 2, z_lo: 2; z = z_hi * 2 + z_lo), core: 2. Of those that a mesh axis runs over, the one named last changes fastest.
Arguments:
- tokens: bfloat16 [12288, 1024], P(('wide', 'narrow')), may hold values from -6 to 6
- cotangent: bfloat16 [12288, 1024], P(('wide', 'narrow')), may hold values from -6 to 6
- segments: int32 [16, 768], P('wide'), may hold values from 0 to 3, never falling along the last dimension, each value on 1 to 384 neighbouring positions
- w_query: bfloat16 [1024, 1024], P(None, 'narrow'), may hold values from -0.1875 to 0.1875
- w_key: bfloat16 [1024, 1024], P(None, 'narrow'), may hold values from -0.1875 to 0.1875
- w_value: bfloat16 [1024, 1024], P(None, 'narrow'), may hold values from -0.1875 to 0.1875
- w_out: bfloat16 [1024, 1024], P('narrow'), may hold values from -1.5 to 1.5
- w_gate: bfloat16 [1024, 4096], P(None, 'narrow'), may hold values from -0.1875 to 0.1875
- w_up: bfloat16 [1024, 4096], P(None, 'narrow'), may hold values from -0.1875 to 0.1875
- w_down: bfloat16 [4096, 1024], P('narrow'), may hold values from -0.09375 to 0.09375
- gain_one: float32 [1024], replicated, may hold values from 0.25 to 1.75
- bias_one: float32 [1024], replicated, may hold values from -2.5 to 2.5
- gain_two: float32 [1024], replicated, may hold values from 0.25 to 1.75
- bias_two: float32 [1024], replicated, may hold values from -2.5 to 2.5
Outputs:
- layer_out: float32 [12288, 1024], P(('wide', 'narrow'))
- input_grad: float32 [12288, 1024], P(('wide', 'narrow'))
- grad_query: float32 [1024, 1024], P(None, 'narrow')
- grad_key: float32 [1024, 1024], P(None, 'narrow')
- grad_value: float32 [1024, 1024], P(None, 'narrow')
- grad_out: float32 [1024, 1024], P('narrow')
- grad_gate: float32 [1024, 4096], P(None, 'narrow')
- grad_up: float32 [1024, 4096], P(None, 'narrow')
- grad_down: float32 [4096, 1024], P('narrow')
- grad_gain_one: float32 [1024], replicated
- grad_bias_one: float32 [1024], replicated
- grad_gain_two: float32 [1024], replicated
- grad_bias_two: float32 [1024], replicated
Inputs may be any that keep to these rules, and one draw needn't show every extreme that they name: `segments`: within each row of 768 tokens segment numbers never fall; each segment holds 1 to 384 tokens and one holds exactly 384.
All inputs are finite; a program needn't handle non-finite values.
Results may differ from a plain program's by a relative error of at most 0.03.
Values may be sent and summed in bfloat16 or wider, within the bound.
No kernel may reach another device: no remote copies, remote signals or barrier semaphores. Data moves between devices by JAX's collectives and lax.ppermute only.
A program may use at most 128 MiB of HBM per device.

v0:
```python
import math
import jax
import jax.numpy as jnp
from jax import lax
from jax.sharding import PartitionSpec as P

HD = 64
EPS = 1e-05
MASKED = -1e30


def normalize(values, gain_vec, bias_vec):
    centred = values - jnp.mean(values, axis=-1, keepdims=True)
    inverse = lax.rsqrt(jnp.mean(centred * centred, axis=-1, keepdims=True) + EPS)
    scaled = centred * inverse
    return (scaled * gain_vec + bias_vec, scaled, inverse)


def normalize_back(grad_in, scaled, inverse, gain_vec):
    along = grad_in * gain_vec
    return inverse * (
        along
        - jnp.mean(along, axis=-1, keepdims=True)
        - scaled * jnp.mean(along * scaled, axis=-1, keepdims=True)
    )


def contract_last(left_side, right_side):
    return lax.dot_general(
        left_side, right_side, (((1,), (1,)), ((), ())), preferred_element_type=jnp.float32
    )


def contract_first(left_side, right_side):
    return lax.dot_general(
        left_side, right_side, (((0,), (0,)), ((), ())), preferred_element_type=jnp.float32
    )


def rotary_tables(seg_rows):
    length = seg_rows.shape[-1]
    column = lax.broadcasted_iota(jnp.int32, (length, length), 1)
    row_index = lax.broadcasted_iota(jnp.int32, (length,), 0)
    same_segment = seg_rows[..., :, None] == seg_rows[..., None, :]
    first_index = jnp.min(jnp.where(same_segment, column, length), axis=-1)
    position = (row_index - first_index).astype(jnp.float32)
    half_width = HD // 2
    inverse = 10000.0 ** (-(2.0 * jnp.arange(half_width).astype(jnp.float32) / HD))
    angles = position[..., None] * inverse
    return (jnp.cos(angles), jnp.sin(angles), same_segment)


def rotate(values, cosine_table, sine_table):
    half_width = values.shape[-1] // 2
    first_half = values[..., :half_width]
    second_half = values[..., half_width:]
    cosine = cosine_table[..., None, :]
    sine_part = sine_table[..., None, :]
    return jnp.concatenate(
        [
            first_half * cosine - second_half * sine_part,
            second_half * cosine + first_half * sine_part,
        ],
        axis=-1,
    )


def unrotate(values, cosine_table, sine_table):
    half_width = values.shape[-1] // 2
    first_half = values[..., :half_width]
    second_half = values[..., half_width:]
    cosine = cosine_table[..., None, :]
    sine_part = sine_table[..., None, :]
    return jnp.concatenate(
        [
            first_half * cosine + second_half * sine_part,
            second_half * cosine - first_half * sine_part,
        ],
        axis=-1,
    )


def project_heads(normed_one, w_query, w_key, w_value, cosine_table, sine_table):
    row_count, length = (cosine_table.shape[0], cosine_table.shape[1])
    head_shape = (row_count, length, w_query.shape[1] // HD, HD)
    queries = rotate(
        jnp.dot(normed_one, w_query, preferred_element_type=jnp.float32).reshape(head_shape),
        cosine_table,
        sine_table,
    ).astype(jnp.bfloat16)
    key_rows = rotate(
        jnp.dot(normed_one, w_key, preferred_element_type=jnp.float32).reshape(head_shape),
        cosine_table,
        sine_table,
    ).astype(jnp.bfloat16)
    value_rows = (
        jnp.dot(normed_one, w_value, preferred_element_type=jnp.float32)
        .astype(jnp.bfloat16)
        .reshape(head_shape)
    )
    return (queries, key_rows, value_rows)


def attention_forward(normed_one, w_query, w_key, w_value, cosine_table, sine_table, same_segment):
    queries, key_rows, value_rows = project_heads(
        normed_one, w_query, w_key, w_value, cosine_table, sine_table
    )
    score_scale = 1.0 / math.sqrt(HD)

    def one_row(row_items):
        query_row, key_row, value_row, mask_row = row_items
        scores = (
            jnp.einsum("qhd,khd->hqk", query_row, key_row, preferred_element_type=jnp.float32)
            * score_scale
        )
        scores = jnp.where(mask_row[None], scores, MASKED)
        row_peak = jnp.max(scores, axis=-1, keepdims=True)
        exponent = jnp.exp(scores - row_peak)
        row_total = jnp.sum(exponent, axis=-1, keepdims=True)
        probs_low = (exponent / row_total).astype(jnp.bfloat16)
        output = jnp.einsum(
            "hqk,khd->qhd", probs_low, value_row, preferred_element_type=jnp.float32
        ).astype(jnp.bfloat16)
        return (output, row_peak + jnp.log(row_total))

    attended, log_total = lax.map(one_row, (queries, key_rows, value_rows, same_segment))
    return (attended.reshape(normed_one.shape[0], -1), log_total)


def attention_grads(
    normed_one,
    attended,
    log_total,
    branch_grad,
    w_query,
    w_key,
    w_value,
    w_out,
    cosine_table,
    sine_table,
    same_segment,
):
    queries, key_rows, value_rows = project_heads(
        normed_one, w_query, w_key, w_value, cosine_table, sine_table
    )
    score_scale = 1.0 / math.sqrt(HD)
    grad_out = contract_first(attended, branch_grad)
    attended_grad = contract_last(branch_grad, w_out).astype(jnp.bfloat16).reshape(queries.shape)

    def one_row(row_items):
        query_row, key_row, value_row, mask_row, total_row, grad_row = row_items
        scores = (
            jnp.einsum("qhd,khd->hqk", query_row, key_row, preferred_element_type=jnp.float32)
            * score_scale
        )
        scores = jnp.where(mask_row[None], scores, MASKED)
        probs = jnp.exp(scores - total_row)
        probs_low = probs.astype(jnp.bfloat16)
        prob_grad = jnp.einsum(
            "qhd,khd->hqk", grad_row, value_row, preferred_element_type=jnp.float32
        )
        score_grad = (
            probs * (prob_grad - jnp.sum(probs * prob_grad, axis=-1, keepdims=True))
        ).astype(jnp.bfloat16)
        query_grad = score_scale * jnp.einsum(
            "hqk,khd->qhd", score_grad, key_row, preferred_element_type=jnp.float32
        )
        key_grad = score_scale * jnp.einsum(
            "hqk,qhd->khd", score_grad, query_row, preferred_element_type=jnp.float32
        )
        value_grad = jnp.einsum(
            "hqk,qhd->khd", probs_low, grad_row, preferred_element_type=jnp.float32
        ).astype(jnp.bfloat16)
        return (query_grad, key_grad, value_grad)

    query_grad, key_grad, value_grad = lax.map(
        one_row, (queries, key_rows, value_rows, same_segment, log_total, attended_grad)
    )
    token_count = normed_one.shape[0]
    query_grad = (
        unrotate(query_grad, cosine_table, sine_table).astype(jnp.bfloat16).reshape(token_count, -1)
    )
    key_grad = (
        unrotate(key_grad, cosine_table, sine_table).astype(jnp.bfloat16).reshape(token_count, -1)
    )
    value_grad = value_grad.reshape(token_count, -1)
    grad_query = contract_first(normed_one, query_grad)
    grad_key = contract_first(normed_one, key_grad)
    grad_value = contract_first(normed_one, value_grad)
    partial_sum = (
        contract_last(query_grad, w_query)
        + contract_last(key_grad, w_key)
        + contract_last(value_grad, w_value)
    )
    return (partial_sum, grad_query, grad_key, grad_value, grad_out)


def swiglu(normed_two, w_gate, w_up):
    gate_pre = jnp.dot(normed_two, w_gate, preferred_element_type=jnp.float32)
    up_pre = jnp.dot(normed_two, w_up, preferred_element_type=jnp.float32)
    sigmoid_gate = jax.nn.sigmoid(gate_pre)
    active = gate_pre * sigmoid_gate
    hidden = (active * up_pre).astype(jnp.bfloat16)
    return (hidden, gate_pre, up_pre, sigmoid_gate, active)


def swiglu_grads(normed_two, out_grad, w_gate, w_up, w_down):
    hidden, gate_pre, up_pre, sigmoid_gate, active = swiglu(normed_two, w_gate, w_up)
    hidden_grad = contract_last(out_grad, w_down)
    grad_down = contract_first(hidden, out_grad)
    gate_grad = (
        hidden_grad * up_pre * sigmoid_gate * (1.0 + gate_pre * (1.0 - sigmoid_gate))
    ).astype(jnp.bfloat16)
    up_grad = (hidden_grad * active).astype(jnp.bfloat16)
    grad_gate = contract_first(normed_two, gate_grad)
    grad_up = contract_first(normed_two, up_grad)
    partial_sum = contract_last(gate_grad, w_gate) + contract_last(up_grad, w_up)
    return (partial_sum, grad_gate, grad_up, grad_down)


def per_device(
    tokens,
    cotangent,
    segments,
    w_query,
    w_key,
    w_value,
    w_out,
    w_gate,
    w_up,
    w_down,
    gain_one,
    bias_one,
    gain_two,
    bias_two,
):
    shard_rows = tokens.shape[0]
    narrow_index = lax.axis_index("narrow")
    cosine_table, sine_table, same_segment = rotary_tables(segments)
    gathered, cot_whole = (
        lax.all_gather(tokens, "narrow", axis=0, tiled=True),
        lax.all_gather(cotangent, "narrow", axis=0, tiled=True),
    )
    inputs = gathered.astype(jnp.float32)
    normed_float, scaled_one, inverse_one = normalize(inputs, gain_one, bias_one)
    normed_one = normed_float.astype(jnp.bfloat16)
    attended, log_total = attention_forward(
        normed_one, w_query, w_key, w_value, cosine_table, sine_table, same_segment
    )
    middle = inputs + lax.psum(
        jnp.dot(attended, w_out, preferred_element_type=jnp.float32).astype(jnp.bfloat16), "narrow"
    ).astype(jnp.float32)
    normed_float_two, scaled_two, inverse_two = normalize(middle, gain_two, bias_two)
    normed_two = normed_float_two.astype(jnp.bfloat16)
    hidden = swiglu(normed_two, w_gate, w_up)[0]
    result_whole = middle + lax.psum(
        jnp.dot(hidden, w_down, preferred_element_type=jnp.float32).astype(jnp.bfloat16), "narrow"
    ).astype(jnp.float32)
    layer_out = lax.dynamic_slice_in_dim(result_whole, narrow_index * shard_rows, shard_rows, 0)
    partial_two, grad_gate, grad_up, grad_down = swiglu_grads(
        normed_two, cot_whole, w_gate, w_up, w_down
    )
    normed_two_grad = lax.psum(partial_two.astype(jnp.bfloat16), "narrow").astype(jnp.float32)
    middle_grad = cot_whole.astype(jnp.float32) + normalize_back(
        normed_two_grad, scaled_two, inverse_two, gain_two
    )
    own_two_grad = lax.dynamic_slice_in_dim(
        normed_two_grad, narrow_index * shard_rows, shard_rows, 0
    )
    own_scaled_two = lax.dynamic_slice_in_dim(scaled_two, narrow_index * shard_rows, shard_rows, 0)
    branch_grad = middle_grad.astype(jnp.bfloat16)
    partial_one, grad_query, grad_key, grad_value, grad_out = attention_grads(
        normed_one,
        attended,
        log_total,
        branch_grad,
        w_query,
        w_key,
        w_value,
        w_out,
        cosine_table,
        sine_table,
        same_segment,
    )
    normed_one_grad = lax.psum(partial_one.astype(jnp.bfloat16), "narrow").astype(jnp.float32)
    input_whole = middle_grad + normalize_back(normed_one_grad, scaled_one, inverse_one, gain_one)
    input_grad = lax.dynamic_slice_in_dim(input_whole, narrow_index * shard_rows, shard_rows, 0)
    own_one_grad = lax.dynamic_slice_in_dim(
        normed_one_grad, narrow_index * shard_rows, shard_rows, 0
    )
    own_scaled_one = lax.dynamic_slice_in_dim(scaled_one, narrow_index * shard_rows, shard_rows, 0)
    matrices = (
        lax.psum(grad_query.astype(jnp.bfloat16), "wide").astype(jnp.float32),
        lax.psum(grad_key.astype(jnp.bfloat16), "wide").astype(jnp.float32),
        lax.psum(grad_value.astype(jnp.bfloat16), "wide").astype(jnp.float32),
        lax.psum(grad_out.astype(jnp.bfloat16), "wide").astype(jnp.float32),
        lax.psum(grad_gate.astype(jnp.bfloat16), "wide").astype(jnp.float32),
        lax.psum(grad_up.astype(jnp.bfloat16), "wide").astype(jnp.float32),
        lax.psum(grad_down.astype(jnp.bfloat16), "wide").astype(jnp.float32),
    )
    norm_grads = lax.psum(
        (
            jnp.sum(own_one_grad * own_scaled_one, axis=0),
            jnp.sum(own_one_grad, axis=0),
            jnp.sum(own_two_grad * own_scaled_two, axis=0),
            jnp.sum(own_two_grad, axis=0),
        ),
        ("wide", "narrow"),
    )
    return (
        layer_out,
        input_grad,
        matrices[0],
        matrices[1],
        matrices[2],
        matrices[3],
        matrices[4],
        matrices[5],
        matrices[6],
        norm_grads[0],
        norm_grads[1],
        norm_grads[2],
        norm_grads[3],
    )


def solution(mesh):
    placed = (
        P(("wide", "narrow"), None),
        P(("wide", "narrow"), None),
        P("wide", None),
        P(None, "narrow"),
        P(None, "narrow"),
        P(None, "narrow"),
        P("narrow", None),
        P(None, "narrow"),
        P(None, "narrow"),
        P("narrow", None),
        P(),
        P(),
        P(),
        P(),
    )
    return jax.shard_map(
        per_device,
        mesh=mesh,
        in_specs=placed,
        out_specs=(
            P(("wide", "narrow"), None),
            P(("wide", "narrow"), None),
            P(None, "narrow"),
            P(None, "narrow"),
            P(None, "narrow"),
            P("narrow", None),
            P(None, "narrow"),
            P(None, "narrow"),
            P("narrow", None),
            P(),
            P(),
            P(),
            P(),
        ),
        check_vma=False,
    )
```

profile of v0, /device:TPU:0, one launch (start us, length us, event | category | flops | bytes accessed | tf_op | source)
XLA Modules:
  0.0 550.6 jit_solution(14009956408082012891)
XLA Ops:
  10.9 41.9 %all-gather.3.cloned.1.call-done = bf16[768,1024]{1,0:T(8,128)(2,1)} async-done(((bf16[96,1024]{1,0:T(8,128)(2,1)}), bf16[768,1024]{1,0:T(8,128)(2,1)}) %all-gather.3.cloned.1.call-update) | async-done | bytes 1572880 | tf_op jit(solution)/shard_map/all_gather | solution.py:241
  54.6 2.0 fusion.4
  66.2 77.9 %all-reduce.8.cloned.1.call-done = bf16[768,1024]{1,0:T(8,128)(2,1)} async-done(((bf16[768,1024]{1,0:T(8,128)(2,1)}), bf16[768,1024]{1,0:T(8,128)(2,1)}) %all-reduce.8.cloned.1.call-update) | async-done | bytes 1572880 | tf_op jit(solution)/shard_map/psum | solution.py:250
  144.1 2.0 fusion.28
  146.9 3.6 add_convert_fusion.2
  150.4 2.1 fusion.32
  152.6 2.1 fusion.33
  154.7 31.3 %all-gather.5.cloned.1.call-done = bf16[768,1024]{1,0:T(8,128)(2,1)} async-done(((bf16[96,1024]{1,0:T(8,128)(2,1)}), bf16[768,1024]{1,0:T(8,128)(2,1)}) %all-gather.5.cloned.1.call-update) | async-done | bytes 1572880 | tf_op jit(solution)/shard_map/all_gather | solution.py:242
  185.9 5.0 multiply_convert_fusion.1
  192.7 2.2 add_convert_fusion.1
  195.2 3.3 convolution_convert_fusion
  198.4 75.3 %all-reduce.10.cloned.1.call-done = bf16[768,1024]{1,0:T(8,128)(2,1)} async-done(((bf16[768,1024]{1,0:T(8,128)(2,1)}), bf16[768,1024]{1,0:T(8,128)(2,1)}) %all-reduce.10.cloned.1.call-update) | async-done | bytes 1572880 | tf_op jit(solution)/shard_map/psum | solution.py:263
  273.7 3.2 multiply_reduce_fusion.4
  277.5 2.6 multiply_add_fusion
  288.8 3.7 convolution_convert_fusion.3
  292.6 2.0 convolution_convert_fusion.4
  294.6 2.0 convolution_convert_fusion.2
  301.8 3.4 convert_element_type.182
  305.2 73.7 %all-reduce.14.cloned.1.call-done = (bf16[768,1024]{1,0:T(8,128)(2,1)}, bf16[768,1024]{1,0:T(8,128)(2,1)}) async-done(((bf16[768,1024]{1,0:T(8,128)(2,1)}, bf16[768,1024]{1,0:T(8,128)(2,1)}), (bf16[768,1024]{1,0:T(8,128)(2,1)}, bf16[768,1024]{1,0:T(8,128)(2,1)})) %all-reduce.14.cloned.1.call-update) | async-done | bytes 3145744 | tf_op jit(solution)/shard_map/psum | solution.py:256
  378.9 1.9 convert_element_type.192
  382.2 2.2 dynamic-slice_reduce_fusion
  384.4 65.4 %all-reduce = (f32[1024]{0:T(1024)}, f32[1024]{0:T(1024)}, f32[1024]{0:T(1024)}, f32[1024]{0:T(1024)}) all-reduce(f32[1024]{0:T(1024)S(1)} %get-tuple-element.113, f32[1024]{0:T(1024)S(1)} %get-tuple-element.114, f32[1024]{0:T(1024)S(1)} %get-tuple-element.55, ...), channel_id=1, replica_groups=mesh['wide'=16,'narrow'=8] {'wide','narrow'}, use_global_device_ids=true, to_apply=%region_24.25 | all-reduce | flops 4096 | bytes 32768 | tf_op jit(solution)/shard_map/psum | solution.py:301
  451.6 82.6 %all-reduce.12.cloned.1.call-done = (bf16[1024,128]{1,0:T(8,128)(2,1)}, bf16[1024,128]{1,0:T(8,128)(2,1)}, bf16[1024,128]{1,0:T(8,128)(2,1)}, bf16[128,1024]{1,0...) async-done(((bf16[1024,128]{1,0:T(8,128)(2,1)}, bf16[1024,128]{1,0:T(8,128)(2,1)}, bf16[1024,128]{1,0:T(8,128)(2,1)}, ...) | async-done | bytes 4194320 | tf_op jit(solution)/shard_map/psum | solution.py:293
  534.2 3.0 convert_element_type.202
  (177 shorter events, 41.7 us)
Async XLA Ops:
  7.2 178.8 %copy-start = (bf16[512,1024]{1,0:T(8,128)(2,1)S(1)}, bf16[512,1024]{1,0:T(8,128)(2,1)}, u32[]{:S(2)}) copy-start(bf16[512,1024]{1,0:T(8,128)(2,1)} %param.23) | copy-start | bytes 3145732
  7.2 49.4 %copy-start.49 = (f32[1024]{0:T(1024)S(1)}, f32[1024]{0:T(1024)}, u32[]{:S(2)}) copy-start(f32[1024]{0:T(1024)} %param.24) | copy-start | bytes 12292
  7.2 49.4 %copy-start.50 = (f32[1024]{0:T(1024)S(1)}, f32[1024]{0:T(1024)}, u32[]{:S(2)}) copy-start(f32[1024]{0:T(1024)} %param.25) | copy-start | bytes 12292
  7.2 45.6 %all-gather.3.cloned.1.call-start = ((), (), s32[]{:S(2)}) async-start(), calls=%async_computation | async-start | bytes 1769472 | tf_op jit(solution)/shard_map/all_gather | solution.py:241
  8.0 136.2 %all-reduce.8.cloned.1.call-start = ((), (), s32[]{:S(2)}) async-start(), calls=%async_computation.1 | async-start | bytes 3145728 | tf_op jit(solution)/shard_map/psum | solution.py:250
  9.7 49.7 %copy-start.26 = (f32[768,32]{0,1:T(8,128)}, f32[768,32]{0,1:T(8,128)S(1)}, u32[]{:S(2)}) copy-start(f32[768,32]{0,1:T(8,128)S(1)} %get-tuple-element.107) | copy-start | bytes 294916
  10.9 46.4 %copy-start.22 = (bf16[1024,128]{1,0:T(8,128)(2,1)S(1)}, bf16[1024,128]{1,0:T(8,128)(2,1)}, u32[]{:S(2)}) copy-start(bf16[1024,128]{1,0:T(8,128)(2,1)} %param.17) | copy-start | bytes 786436
  52.8 3.9 copy-start.2
  65.2 120.7 %all-gather.5.cloned.1.call-start = ((), (), s32[]{:S(2)}) async-start(), calls=%async_computation.2 | async-start | bytes 1769472 | tf_op jit(solution)/shard_map/all_gather | solution.py:242
  66.0 80.9 %copy-start.48 = (f32[1024]{0:T(1024)S(1)}, f32[1024]{0:T(1024)}, u32[]{:S(2)}) copy-start(f32[1024]{0:T(1024)} %param.26) | copy-start | bytes 12292
  66.0 80.9 %copy-start.51 = (f32[1024]{0:T(1024)S(1)}, f32[1024]{0:T(1024)}, u32[]{:S(2)}) copy-start(f32[1024]{0:T(1024)} %param.27) | copy-start | bytes 12292
  66.0 207.7 %all-reduce.10.cloned.1.call-start = ((), (), s32[]{:S(2)}) async-start(), calls=%async_computation.3 | async-start | bytes 3145728 | tf_op jit(solution)/shard_map/psum | solution.py:263
  185.9 5.0 copy-start.16
  194.9 184.0 %all-reduce.14.cloned.1.call-start = ((), (), s32[]{:S(2)}) async-start(), calls=%async_computation.5 | async-start | bytes 6291456 | tf_op jit(solution)/shard_map/psum | solution.py:256
  273.7 3.8 copy-start.9
  273.7 7.0 %slice-start = ((s8[4718592]{0:T(1024)(128)(4,1)}), s8[4194304]{0:T(1024)(128)(4,1)S(1)}, s32[]{:S(2)}) async-start(s8[4718592]{0:T(1024)(128)(4,1)} %bitcast.74), calls=%async_computation.6 | async-start | bytes 8388608
  288.5 4.1 copy-start.29
  288.5 245.7 %all-reduce.12.cloned.1.call-start = ((), (), s32[]{:S(2)}) async-start(), calls=%async_computation.4 | async-start | bytes 8388608 | tf_op jit(solution)/shard_map/psum | solution.py:293
  296.6 4.0 copy-start.7
  296.6 4.0 copy-start.32
  534.2 4.6 copy-start.19
  537.2 4.0 copy-start.46
  538.8 4.1 copy-start.44
  538.8 4.9 copy-start.1
  (37 other events, 73.3 us)
Sparse Core Ops, SparseCore 0:
  9.7 43.0 all-gather.2
  65.4 78.7 all-reduce.7
  145.8 40.1 all-gather.4
  195.0 78.6 all-reduce.9
  288.6 90.2 all-reduce.13
  382.4 151.7 all-reduce.11
where the time goes:
time: 551 us
  waiting for transfers between devices  384 us (70%)
  blocking collectives  65.4 us (12%)
  other arithmetic  41.2 us (7%)
  matrix products  41 us (7%)
  between operations  14.8 us (3%)
    psum x1, waiting for transfers between devices, per_device(): lax.psum(grad_query.astype(jnp.bfloat16), 'wide').astype(jnp.float32)  82.6 us
    psum x1, waiting for transfers between devices, per_device(): lax.psum(jnp.dot(attended, w_out, preferred_element_type=jnp.float32).ast...  77.9 us
    psum x1, waiting for transfers between devices, per_device(): lax.psum(partial_two.astype(jnp.bfloat16), 'narrow').astype(jnp.float32)  75.3 us
    psum x1, waiting for transfers between devices, per_device(): lax.psum(jnp.dot(hidden, w_down, preferred_element_type=jnp.float32).asty...  73.7 us
    psum x1, blocking collectives, per_device(): lax.psum((jnp.sum(own_one_grad * own_scaled_one, axis=0), jnp.sum(own_one...  65.4 us
    all_gather x1, waiting for transfers between devices, per_device(): lax.all_gather(tokens, 'narrow', axis=0, tiled=True)  41.9 us
    all_gather x1, waiting for transfers between devices, per_device(): lax.all_gather(cotangent, 'narrow', axis=0, tiled=True)  31.3 us
    dot_general x7, matrix products, contract_first(): lax.dot_general(left_side, right_side, (((0,), (0,)), ((), ())), preferre...  12.8 us
  transfers between devices with their start and end apart: 6, of which 6 were waited for; matrix products, arithmetic and copies ran while one was open for 7% of the time, Pallas kernels for 0%

commit v1 on v0

--- a/solution.py
+++ b/solution.py
@@ -3,6 +3,7 @@
 import jax.numpy as jnp
 from jax import lax
 from jax.sharding import PartitionSpec as P
+from jax.lax import all_to_all, axis_size
 
 HD = 64
 EPS = 1e-05
@@ -237,9 +238,16 @@
     shard_rows = tokens.shape[0]
     narrow_index = lax.axis_index("narrow")
     cosine_table, sine_table, same_segment = rotary_tables(segments)
+
+    def prepare_ends_over_axis(vals, dev_axis):
+        oldest = axis_size(dev_axis)
+        even = jnp.stack(oldest * [vals], axis=0)
+        finding = all_to_all(even, dev_axis, 0, 0)
+        return jnp.concatenate(finding, axis=0)
+
     gathered, cot_whole = (
         lax.all_gather(tokens, "narrow", axis=0, tiled=True),
-        lax.all_gather(cotangent, "narrow", axis=0, tiled=True),
+        prepare_ends_over_axis(cotangent, "narrow"),
     )
     inputs = gathered.astype(jnp.float32)
     normed_float, scaled_one, inverse_one = normalize(inputs, gain_one, bias_one)

time: 551 us -> 528 us (0.958)
  waiting for transfers between devices: 384 us -> 353 us
    all_gather x1 -> x0, waiting for transfers between devices: 31.3 us -> none  [per_device(): lax.all_gather(cotangent, 'narrow', axis=0, tiled=True)]
  transfers between devices with their start and end apart: 6 -> 6, of which waited for: 6 -> 5; matrix products, arithmetic and copies ran while one was open for 7% -> 8% of each run, Pallas kernels for 0% -> 0%
where the time goes in v1:
time: 528 us
  waiting for transfers between devices  353 us (67%)
  blocking collectives  65.4 us (12%)
  matrix products  42.5 us (8%)
  other arithmetic  41.2 us (8%)
  between operations  14.5 us (3%)
  local copies, waits for them, and re-layouts  5.51 us (1%)
    psum x1, waiting for transfers between devices, per_device(): lax.psum(grad_query.astype(jnp.bfloat16), 'wide').astype(jnp.float32)  82.6 us
    psum x1, waiting for transfers between devices, per_device(): lax.psum(jnp.dot(attended, w_out, preferred_element_type=jnp.float32).ast...  80.2 us
    psum x1, waiting for transfers between devices, per_device(): lax.psum(partial_two.astype(jnp.bfloat16), 'narrow').astype(jnp.float32)  75.8 us
    psum x1, waiting for transfers between devices, per_device(): lax.psum(jnp.dot(hidden, w_down, preferred_element_type=jnp.float32).asty...  72.2 us
    psum x1, blocking collectives, per_device(): lax.psum((jnp.sum(own_one_grad * own_scaled_one, axis=0), jnp.sum(own_one...  65.4 us
    all_gather x1, waiting for transfers between devices, per_device(): lax.all_gather(tokens, 'narrow', axis=0, tiled=True)  41.9 us
    dot_general x7, matrix products, contract_first(): lax.dot_general(left_side, right_side, (((0,), (0,)), ((), ())), preferre...  14.3 us
    dot_general x7, matrix products, contract_last(): lax.dot_general(left_side, right_side, (((1,), (1,)), ((), ())), preferre...  11.8 us
  transfers between devices with their start and end apart: 6, of which 5 were waited for; matrix products, arithmetic and copies ran while one was open for 8% of the time, Pallas kernels for 0%

profile of v1, /device:TPU:0, one launch (start us, length us, event | category | flops | bytes accessed | tf_op | source)
XLA Modules:
  0.0 527.7 jit_solution(1537145044844240489)
XLA Ops:
  10.9 41.9 %all-gather.2.cloned.1.call-done = bf16[768,1024]{1,0:T(8,128)(2,1)} async-done(((bf16[96,1024]{1,0:T(8,128)(2,1)}), bf16[768,1024]{1,0:T(8,128)(2,1)}) %all-gather.2.cloned.1.call-update) | async-done | bytes 1572880 | tf_op jit(solution)/shard_map/all_gather | solution.py:249
  54.6 2.0 fusion.4
  65.2 2.3 stack.2
  67.5 4.3 all-to-all-start
  72.1 80.2 %all-reduce.8.cloned.1.call-done = bf16[768,1024]{1,0:T(8,128)(2,1)} async-done(((bf16[768,1024]{1,0:T(8,128)(2,1)}), bf16[768,1024]{1,0:T(8,128)(2,1)}) %all-reduce.8.cloned.1.call-update) | async-done | bytes 1572880 | tf_op jit(solution)/shard_map/psum | solution.py:258
  152.3 2.0 fusion.28
  155.0 3.5 add_convert_fusion.2
  158.6 2.1 fusion.32
  160.7 2.1 fusion.33
  162.8 5.0 multiply_convert_fusion.1
  169.6 2.2 add_convert_fusion.1
  172.1 3.3 convolution_convert_fusion
  175.3 75.8 %all-reduce.10.cloned.1.call-done = bf16[768,1024]{1,0:T(8,128)(2,1)} async-done(((bf16[768,1024]{1,0:T(8,128)(2,1)}), bf16[768,1024]{1,0:T(8,128)(2,1)}) %all-reduce.10.cloned.1.call-update) | async-done | bytes 1572880 | tf_op jit(solution)/shard_map/psum | solution.py:271
  251.2 3.2 multiply_reduce_fusion.4
  254.9 2.6 multiply_add_fusion
  266.3 3.7 convolution_convert_fusion.3
  270.0 2.0 convolution_convert_fusion.4
  272.0 3.5 convolution_convert_fusion.2
  280.7 3.5 convert_element_type.182
  284.2 72.2 %all-reduce.14.cloned.1.call-done = (bf16[768,1024]{1,0:T(8,128)(2,1)}, bf16[768,1024]{1,0:T(8,128)(2,1)}) async-done(((bf16[768,1024]{1,0:T(8,128)(2,1)}, bf16[768,1024]{1,0:T(8,128)(2,1)}), (bf16[768,1024]{1,0:T(8,128)(2,1)}, bf16[768,1024]{1,0:T(8,128)(2,1)})) %all-reduce.14.cloned.1.call-update) | async-done | bytes 3145744 | tf_op jit(solution)/shard_map/psum | solution.py:264
  359.6 2.2 dynamic-slice_reduce_fusion
  361.8 65.4 %all-reduce = (f32[1024]{0:T(1024)}, f32[1024]{0:T(1024)}, f32[1024]{0:T(1024)}, f32[1024]{0:T(1024)}) all-reduce(f32[1024]{0:T(1024)S(1)} %get-tuple-element.113, f32[1024]{0:T(1024)S(1)} %get-tuple-element.114, f32[1024]{0:T(1024)S(1)} %get-tuple-element.55, ...), channel_id=1, replica_groups=mesh['wide'=16,'narrow'=8] {'wide','narrow'}, use_global_device_ids=true, to_apply=%region_24.25 | all-reduce | flops 4096 | bytes 32768 | tf_op jit(solution)/shard_map/psum | solution.py:309
  429.0 82.6 %all-reduce.12.cloned.1.call-done = (bf16[1024,128]{1,0:T(8,128)(2,1)}, bf16[1024,128]{1,0:T(8,128)(2,1)}, bf16[1024,128]{1,0:T(8,128)(2,1)}, bf16[128,1024]{1,0...) async-done(((bf16[1024,128]{1,0:T(8,128)(2,1)}, bf16[1024,128]{1,0:T(8,128)(2,1)}, bf16[1024,128]{1,0:T(8,128)(2,1)}, ...) | async-done | bytes 4194320 | tf_op jit(solution)/shard_map/psum | solution.py:301
  511.6 3.0 convert_element_type.202
  (175 shorter events, 42.9 us)
Async XLA Ops:
  7.2 155.7 %copy-start = (bf16[512,1024]{1,0:T(8,128)(2,1)S(1)}, bf16[512,1024]{1,0:T(8,128)(2,1)}, u32[]{:S(2)}) copy-start(bf16[512,1024]{1,0:T(8,128)(2,1)} %param.23) | copy-start | bytes 3145732
  7.2 49.4 %copy-start.48 = (f32[1024]{0:T(1024)S(1)}, f32[1024]{0:T(1024)}, u32[]{:S(2)}) copy-start(f32[1024]{0:T(1024)} %param.24) | copy-start | bytes 12292
  7.2 49.4 %copy-start.49 = (f32[1024]{0:T(1024)S(1)}, f32[1024]{0:T(1024)}, u32[]{:S(2)}) copy-start(f32[1024]{0:T(1024)} %param.25) | copy-start | bytes 12292
  7.2 45.6 %all-gather.2.cloned.1.call-start = ((), (), s32[]{:S(2)}) async-start(), calls=%async_computation.1 | async-start | bytes 1769472 | tf_op jit(solution)/shard_map/all_gather | solution.py:249
  8.0 144.3 %all-reduce.8.cloned.1.call-start = ((), (), s32[]{:S(2)}) async-start(), calls=%async_computation.2 | async-start | bytes 3145728 | tf_op jit(solution)/shard_map/psum | solution.py:258
  9.7 49.7 %copy-start.25 = (f32[768,32]{0,1:T(8,128)}, f32[768,32]{0,1:T(8,128)S(1)}, u32[]{:S(2)}) copy-start(f32[768,32]{0,1:T(8,128)S(1)} %get-tuple-element.107) | copy-start | bytes 294916
  10.9 46.4 %copy-start.21 = (bf16[1024,128]{1,0:T(8,128)(2,1)S(1)}, bf16[1024,128]{1,0:T(8,128)(2,1)}, u32[]{:S(2)}) copy-start(bf16[1024,128]{1,0:T(8,128)(2,1)} %param.17) | copy-start | bytes 786436
  52.8 3.9 copy-start.2
  67.5 95.3 %all-to-all-start = ((bf16[8,96,1024]{2,1,0:T(8,128)(2,1)}), bf16[8,96,1024]{2,1,0:T(8,128)(2,1)}, u32[]{:S(2)}, u32[]{:S(2)}) async-start(bf16[8,96,1024]{2,1,0:T(8,128)(2,1)} %stack.2), calls=%async_computation | async-start | bytes 3145728 | tf_op jit(solution)/shard_map/all_to_all | solution.py:245
  71.8 83.2 %copy-start.47 = (f32[1024]{0:T(1024)S(1)}, f32[1024]{0:T(1024)}, u32[]{:S(2)}) copy-start(f32[1024]{0:T(1024)} %param.26) | copy-start | bytes 12292
  71.8 83.2 %copy-start.50 = (f32[1024]{0:T(1024)S(1)}, f32[1024]{0:T(1024)}, u32[]{:S(2)}) copy-start(f32[1024]{0:T(1024)} %param.27) | copy-start | bytes 12292
  71.8 179.3 %all-reduce.10.cloned.1.call-start = ((), (), s32[]{:S(2)}) async-start(), calls=%async_computation.3 | async-start | bytes 3145728 | tf_op jit(solution)/shard_map/psum | solution.py:271
  162.8 5.0 copy-start.15
  171.8 184.5 %all-reduce.14.cloned.1.call-start = ((), (), s32[]{:S(2)}) async-start(), calls=%async_computation.5 | async-start | bytes 6291456 | tf_op jit(solution)/shard_map/psum | solution.py:264
  251.2 3.8 copy-start.9
  251.2 7.0 %slice-start = ((s8[4718592]{0:T(1024)(128)(4,1)}), s8[4194304]{0:T(1024)(128)(4,1)S(1)}, s32[]{:S(2)}) async-start(s8[4718592]{0:T(1024)(128)(4,1)} %bitcast.76), calls=%async_computation.6 | async-start | bytes 8388608
  266.0 4.1 copy-start.28
  266.0 245.7 %all-reduce.12.cloned.1.call-start = ((), (), s32[]{:S(2)}) async-start(), calls=%async_computation.4 | async-start | bytes 8388608 | tf_op jit(solution)/shard_map/psum | solution.py:301
  275.5 4.0 copy-start.7
  275.5 4.0 copy-start.31
  511.6 4.6 copy-start.18
  514.6 4.0 copy-start.45
  516.2 4.1 copy-start.43
  516.2 4.9 copy-start.1
  (36 other events, 72.7 us)
Sparse Core Ops, SparseCore 0:
  9.7 43.0 all-gather.1
  65.4 86.8 all-reduce.7
  171.9 79.2 all-reduce.9
  266.1 90.1 all-reduce.13
  359.8 151.7 all-reduce.11
